TPU v7x, 32 devices: a whole 2x2x4 slice. The times are simulated.
32 devices in a mesh: layer: 8 (over z, x), land: 4 (over y, core).
Axes of the slice: x: 2, y: 2, z: 4, core: 2. Of those that a mesh axis runs over, the one named last changes fastest.
Arguments:
- gradients: bfloat16 [960, 65536], P(None, ('layer', 'land')), may hold values from -6 to 6
- queries: bfloat16 [32, 65536], P(None, ('layer', 'land')), may hold values from -6 to 6
- landmarks: bfloat16 [1024, 65536], P(None, ('layer', 'land')), may hold values from -0.0234375 to 0.0234375
- whitening: bfloat16 [1024, 1024], P(None, 'land'), may hold values from -2.5 to 2.5
Outputs:
- scores: float32 [32, 960], P('land', 'layer')
All inputs are finite; a program needn't handle non-finite values.
Results may differ from a plain program's by a relative error of at most 0.023.
Values may be sent and summed in bfloat16 or wider, within the bound.
A program may use at most 128 MiB of HBM per device.

v0:
```python
import jax
import jax.numpy as jnp
from jax import lax
from jax.sharding import PartitionSpec as P

LANDMARKS = 1024


def contract_rows(rows, piece):
    return lax.dot_general(
        rows, piece, (((1,), (1,)), ((), ())), preferred_element_type=jnp.float32
    )


def make_folder(example_rows, query_rows, piece):
    return (contract_rows(example_rows, piece), contract_rows(query_rows, piece))


def local(gradients, queries, landmarks, whitening):
    n_layer = lax.axis_size("layer")
    n_land = lax.axis_size("land")
    width = gradients.shape[1]
    rows_each = gradients.shape[0] // (n_layer * n_land)
    query_each = queries.shape[0] // (n_layer * n_land)
    split_ex = gradients.reshape(n_layer, n_land, rows_each, width)
    split_qr = queries.reshape(n_layer, n_land, query_each, width)
    moved_ex, moved_qr = (
        lax.all_to_all(split_ex, "land", split_axis=1, concat_axis=3, tiled=True),
        lax.all_to_all(split_qr, "land", split_axis=1, concat_axis=3, tiled=True),
    )
    layer_rows = moved_ex.reshape(n_layer * rows_each, n_land * width)
    layer_query = moved_qr.reshape(n_layer * query_each, n_land * width)
    partial_ex, partial_qr = make_folder(
        layer_rows, layer_query, lax.all_gather(landmarks, "land", axis=1, tiled=True)
    )
    share_ex, share_qr = (
        lax.psum_scatter(
            partial_ex.astype(jnp.bfloat16), "layer", scatter_dimension=0, tiled=True
        ).astype(jnp.float32),
        lax.psum_scatter(
            partial_qr.astype(jnp.bfloat16), "layer", scatter_dimension=0, tiled=True
        ).astype(jnp.float32),
    )
    projected, query_proj = (
        lax.all_gather(share_ex.astype(jnp.bfloat16), "land", axis=0, tiled=True),
        lax.all_gather(share_qr.astype(jnp.bfloat16), "land", axis=0, tiled=True),
    )
    whitened = jnp.dot(projected, whitening, preferred_element_type=jnp.float32).astype(
        jnp.bfloat16
    )
    query_white = jnp.dot(query_proj, whitening, preferred_element_type=jnp.float32).astype(
        jnp.bfloat16
    )
    all_queries = lax.all_gather(query_white, "layer", axis=0, tiled=True)
    factor = LANDMARKS ** (-0.5)
    return lax.psum_scatter(
        (contract_rows(all_queries, whitened) * factor).astype(jnp.bfloat16),
        "land",
        scatter_dimension=0,
        tiled=True,
    ).astype(jnp.float32)


def solution(mesh):
    return jax.shard_map(
        local,
        mesh=mesh,
        in_specs=(
            P(None, ("layer", "land")),
            P(None, ("layer", "land")),
            P(None, ("layer", "land")),
            P(None, "land"),
        ),
        out_specs=P("land", "layer"),
        check_vma=False,
    )
```

profile of v0, /device:TPU:0, one launch (start us, length us, event | category | flops | bytes accessed | tf_op | source)
XLA Modules:
  0.0 296.0 jit_solution(8832669708729953579)
XLA Ops:
  6.5 0.7 all-gather.5.cloned.1.call-update
  7.3 5.0 %reshape.19 = bf16[8,4,30,2048]{3,2,1,0:T(8,128)(2,1)} reshape(bf16[960,2048]{1,0:T(8,128)(2,1)} %param.4) | data formatting | bytes 7864320 | tf_op jit(solution)/shard_map/reshape | solution.py:25
  12.3 6.4 %copy.9 = bf16[8,4,30,2048]{3,0,2,1:T(8,128)(2,1)} copy(bf16[8,4,30,2048]{3,2,1,0:T(8,128)(2,1)} %reshape.19) | data formatting | bytes 7864320 | tf_op jit(solution)/shard_map/reshape | solution.py:25
  18.7 5.1 %all-to-all-start.1 = ((bf16[8,4,30,2048]{3,0,2,1:T(8,128)(2,1)}), bf16[8,4,30,2048]{3,0,2,1:T(8,128)(2,1)}, u32[]{:S(2)}, u32[]{:S(2)}) async-start(bf16[8,4,30,2048]{3,0,2,1:T(8,128)(2,1)} %copy.9), calls=%async_computation.1 | async-start | bytes 7864320 | tf_op jit(solution)/shard_map/all_to_all | solution.py:28
  23.9 0.7 copy.8
  24.6 0.6 dynamic-slice.4
  25.2 0.7 fusion.7
  27.1 85.5 %all-to-all-done.1 = bf16[8,4,30,2048]{3,0,2,1:T(8,128)(2,1)} async-done(((bf16[8,4,30,2048]{3,0,2,1:T(8,128)(2,1)}), bf16[8,4,30,2048]{3,0,2,1:T(8,128)(2,1)}, u32[]{:S(2)}, u32[]{:S(2)}) %all-to-all-start.1) | async-done | bytes 3932192 | tf_op jit(solution)/shard_map/all_to_all | solution.py:28
  112.6 3.5 %all-to-all-start = ((bf16[8,4,1,2048]{3,0,2,1:T(8,128)(2,1)}), bf16[8,4,1,2048]{3,0,2,1:T(8,128)(2,1)S(1)}, u32[]{:S(2)}, u32[]{:S(2)}) async-start(bf16[8,4,1,2048]{3,0,2,1:T(8,128)(2,1)} %copy.8), calls=%async_computation | async-start | bytes 262144 | tf_op jit(solution)/shard_map/all_to_all | solution.py:29
  116.1 5.1 %copy.10 = bf16[8,1,30,4,2048]{4,3,2,0,1:T(4,128)(2,1)S(1)} copy(bf16[8,1,30,4,2048]{4,0,2,3,1:T(8,128)(2,1)} %bitcast.4) | data formatting | bytes 7864320 | tf_op jit(solution)/shard_map/all_to_all | solution.py:28
  121.2 6.0 %copy.12 = bf16[30,8,4,2048]{3,1,2,0:T(8,128)(2,1)} copy(bf16[30,8,4,2048]{3,2,1,0:T(4,128)(2,1)S(1)} %bitcast.29) | data formatting | bytes 7864320
  127.2 33.9 %all-gather.5.cloned.1.call-done = bf16[1024,8192]{1,0:T(8,128)(2,1)} async-done(((bf16[1024,2048]{1,0:T(8,128)(2,1)}), bf16[1024,8192]{1,0:T(8,128)(2,1)}) %all-gather.5.cloned.1.call-update) | async-done | bytes 16777232 | tf_op jit(solution)/shard_map/all_gather | solution.py:34
  161.1 11.5 %convolution_convert_fusion = bf16[240,1024]{1,0:T(8,128)(2,1)S(1)} fusion(bf16[240,8192]{1,0:T(8,128)(2,1)} %bitcast.30, bf16[1024,8192]{1,0:T(8,128)(2,1)} %all-gather.5.cloned.1.call-done), kind=kOutput, calls=%fused_computation | convolution fusion | flops 4026777600 | bytes 21200896 | tf_op jit(solution)/shard_map/dot_general | solution.py:10
  172.6 25.3 %fusion = bf16[32,1024]{1,0:T(8,128)(2,1)S(1)} fusion(bf16[240,1024]{1,0:T(8,128)(2,1)S(1)} %convolution_convert_fusion), kind=kCustom, calls=%all-reduce-scatter | all-reduce-scatter fusion | flops 262145 | bytes 557568
  197.9 2.1 collective-permute-start
  200.0 10.2 %convolution_convert_fusion.2 = bf16[8,1024]{1,0:T(8,128)(2,1)S(1)} fusion(bf16[8,8192]{1,0:T(8,128)(2,1)S(1)} %bitcast.31, bf16[1024,8192]{1,0:T(8,128)(2,1)} %all-gather.5.cloned.1.call-done), kind=kOutput, calls=%fused_computation.3 | convolution fusion | flops 134225920 | bytes 16924672 | tf_op jit(solution)/shard_map/dot_general | solution.py:10
  210.2 33.6 %all-reduce = bf16[8,1024]{1,0:T(8,128)(2,1)S(1)} all-reduce(bf16[8,1024]{1,0:T(8,128)(2,1)S(1)} %convolution_convert_fusion.2), channel_id=2, replica_groups=mesh['layer'=8,'land'=4] {'layer'}, use_global_device_ids=true, to_apply=%region_0.0.clone | all-reduce | flops 8192 | bytes 32768
  243.8 0.6 dynamic-slice_bitcast_fusion.1
  244.4 5.2 %all-gather = bf16[4,1,1024]{2,1,0:T(2,128)(2,1)S(1)} all-gather(bf16[1,1,1024]{2,1,0:T(2,128)(2,1)S(1)} %dynamic-slice_bitcast_fusion.1), channel_id=1, replica_groups=mesh['layer'=8,'land'=4] {'land'}, dimensions={0}, use_global_device_ids=true | all-gather | bytes 10240 | tf_op jit(solution)/shard_map/all_gather | solution.py:46
  249.8 26.0 %all-gather.1 = bf16[8,4,256]{2,1,0:T(4,128)(2,1)S(1)} all-gather(bf16[1,4,256]{2,1,0:T(4,128)(2,1)S(1)} %fusion.4), channel_id=1, replica_groups=mesh['layer'=8,'land'=4] {'layer'}, dimensions={0}, use_global_device_ids=true | all-gather | bytes 18432 | tf_op jit(solution)/shard_map/all_gather | solution.py:54
  276.1 5.8 %all-gather.2 = bf16[4,30,1024]{2,1,0:T(8,128)(2,1)S(1)} all-gather(bf16[1,30,1024]{2,1,0:T(8,128)(2,1)S(1)} %dynamic-slice_bitcast_fusion), channel_id=1, replica_groups=mesh['layer'=8,'land'=4] {'land'}, dimensions={0}, use_global_device_ids=true | all-gather | bytes 307200 | tf_op jit(solution)/shard_map/all_gather | solution.py:45
  281.9 0.3 fusion.3
  282.3 6.2 %all-reduce.2 = bf16[32,120]{1,0:T(8,128)(2,1)S(1)} all-reduce(bf16[32,120]{1,0:T(8,128)(2,1)S(1)} %fusion.3), channel_id=4, replica_groups=mesh['layer'=8,'land'=4] {'land'}, use_global_device_ids=true, to_apply=%region_2.0.clone | all-reduce | flops 3840 | bytes 15360
  288.5 0.6 dynamic-slice_convert_fusion
  (18 shorter events, 0.6 us)
Async XLA Ops:
  6.5 243.1 %copy-start = (bf16[1024,256]{1,0:T(8,128)(2,1)S(1)}, bf16[1024,256]{1,0:T(8,128)(2,1)}, u32[]{:S(2)}) copy-start(bf16[1024,256]{1,0:T(8,128)(2,1)} %param.7) | copy-start | bytes 1572868
  6.5 154.6 %all-gather.5.cloned.1.call-start = ((), (), s32[]{:S(2)}) async-start(), calls=%async_computation.2 | async-start | bytes 20971520 | tf_op jit(solution)/shard_map/all_gather | solution.py:34
  18.7 5.1 %copy-start.1 = (bf16[32,2048]{1,0:T(8,128)(2,1)S(1)}, bf16[32,2048]{1,0:T(8,128)(2,1)}, u32[]{:S(2)}) copy-start(bf16[32,2048]{1,0:T(8,128)(2,1)} %param.5) | copy-start | bytes 393220
  18.7 6.0 %copy-start.3 = (u32[32]{0:T(128)S(1)}, u32[32]{0:T(128)}, u32[]{:S(2)}) copy-start(u32[32]{0:T(128)} %constant.12) | copy-start | bytes 388
  18.7 6.5 %copy-start.2 = (u32[32]{0:T(128)S(1)}, u32[32]{0:T(128)}, u32[]{:S(2)}) copy-start(u32[32]{0:T(128)} %constant.4) | copy-start | bytes 388
  18.7 93.9 %all-to-all-start.1 = ((bf16[8,4,30,2048]{3,0,2,1:T(8,128)(2,1)}), bf16[8,4,30,2048]{3,0,2,1:T(8,128)(2,1)}, u32[]{:S(2)}, u32[]{:S(2)}) async-start(bf16[8,4,30,2048]{3,0,2,1:T(8,128)(2,1)} %copy.9), calls=%async_computation.1 | async-start | bytes 7864320 | tf_op jit(solution)/shard_map/all_to_all | solution.py:28
  112.6 87.4 %all-to-all-start = ((bf16[8,4,1,2048]{3,0,2,1:T(8,128)(2,1)}), bf16[8,4,1,2048]{3,0,2,1:T(8,128)(2,1)S(1)}, u32[]{:S(2)}, u32[]{:S(2)}) async-start(bf16[8,4,1,2048]{3,0,2,1:T(8,128)(2,1)} %copy.8), calls=%async_computation | async-start | bytes 262144 | tf_op jit(solution)/shard_map/all_to_all | solution.py:29
  197.9 77.9 %collective-permute-start = (bf16[14,1024]{1,0:T(8,128)(2,1)S(1)}, bf16[14,1024]{1,0:T(8,128)(2,1)S(1)}, u32[]{:S(2)}, u32[]{:S(2)}) collective-permute-start(bf16[14,1024]{1,0:T(8,128)(2,1)S(1)} %slice), channel_id=1, source_target_pairs={{0,4},{4,8},{8,12},{12,16},{16,20},{20,24},{24,28},{1,5},{5,9},{9,... | collective-permute-start | bytes 86024
Sparse Core Ops, SparseCore 0:
  8.9 152.1 all-gather.4
where the time goes:
time: 297 us; the launch traced here: 296 us
  waiting for transfers between devices  120 us (40%)
  blocking collectives  102 us (34%)
  local copies, waits for them, and re-layouts  25.6 us (9%)
  matrix products  22.2 us (7%)
  between operations  14.8 us (5%)
  starting transfers between devices  10.7 us (4%)
    all_to_all x1, waiting for transfers between devices, local(): lax.all_to_all(split_ex, 'land', split_axis=1, concat_axis=3, tiled=True)  85.5 us
    unnamed x3, blocking collectives  65.1 us
    all_gather x1, waiting for transfers between devices, local(): lax.all_gather(landmarks, 'land', axis=1, tiled=True)  33.9 us
    all_gather x1, blocking collectives, local(): all_queries = lax.all_gather(query_white, 'layer', axis=0, tiled=True)  26 us
    dot_general x3, matrix products, contract_rows(): lax.dot_general(rows, piece, (((1,), (1,)), ((), ())), preferred_element_...  22 us
    reshape x2, local copies, waits for them, and re-layouts, local(): split_ex = gradients.reshape(n_layer, n_land, rows_each, width)  11.4 us
    unnamed x17, local copies, waits for them, and re-layouts  8.18 us
  transfers between devices with their start and end apart: 4, of which 2 were waited for; matrix products, arithmetic and copies ran while one was open for 24% of the time, Pallas kernels for 0%

commit v1 on v0

--- a/solution.py
+++ b/solution.py
@@ -2,6 +2,7 @@
 import jax.numpy as jnp
 from jax import lax
 from jax.sharding import PartitionSpec as P
+from jax.lax import axis_index, axis_size, ppermute
 
 LANDMARKS = 1024
 
@@ -30,9 +31,29 @@
     )
     layer_rows = moved_ex.reshape(n_layer * rows_each, n_land * width)
     layer_query = moved_qr.reshape(n_layer * query_each, n_land * width)
-    partial_ex, partial_qr = make_folder(
-        layer_rows, layer_query, lax.all_gather(landmarks, "land", axis=1, tiled=True)
-    )
+
+    def _touch_slices(tile_in):
+        spare = axis_size("land")
+        z1, outer, side_arr = (spare, axis_index("land"), tile_in.shape[1])
+        all_rows = [(k, (k + 1) % z1) for k in range(z1)]
+        kept_rows = [(k, (k - 1) % z1) for k in range(z1)]
+        part_now = jnp.zeros((*tile_in.shape[:1], z1 * side_arr, *tile_in.shape[2:]), tile_in.dtype)
+        part_now = lax.dynamic_update_slice_in_dim(part_now, tile_in, outer * side_arr, axis=1)
+        clean = z1 // 2
+        after = kept_arr = tile_in
+        for dev_i in range(1, clean + 1):
+            after = ppermute(after, "land", all_rows)
+            part_now = lax.dynamic_update_slice_in_dim(
+                part_now, after, (outer - dev_i) % z1 * side_arr, axis=1
+            )
+            if dev_i < z1 - clean:
+                kept_arr = ppermute(kept_arr, "land", kept_rows)
+                part_now = lax.dynamic_update_slice_in_dim(
+                    part_now, kept_arr, (outer + dev_i) % z1 * side_arr, axis=1
+                )
+        return part_now
+
+    partial_ex, partial_qr = make_folder(layer_rows, layer_query, _touch_slices(landmarks))
     share_ex, share_qr = (
         lax.psum_scatter(
             partial_ex.astype(jnp.bfloat16), "layer", scatter_dimension=0, tiled=True

time: 297 us -> 337 us (1.13)
  local copies, waits for them, and re-layouts: 25.6 us -> 46.5 us
  waiting for transfers between devices: 120 us -> 138 us
  starting transfers between devices: 10.7 us -> 27.7 us
  between operations: 14.8 us -> 1.41 us
    ppermute x0 -> x3, waiting for transfers between devices: none -> 88.7 us  [the longest x2 88.7 us: _touch_slices(): after = ppermute(after, 'land', all_rows)]
    all_to_all x1, waiting for transfers between devices: 85.5 us -> 49 us  [local(): lax.all_to_all(split_ex, 'land', split_axis=1, concat_axis=3, tiled=True)]
    all_gather x1 -> x0, waiting for transfers between devices: 33.9 us -> none  [local(): lax.all_gather(landmarks, 'land', axis=1, tiled=True)]
    dynamic_update_slice x0 -> x4, local copies, waits for them, and re-layouts: none -> 16.3 us  [the longest x2 9.39 us: _touch_slices(): lax.dynamic_update_slice_in_dim(part_now, after, (outer - dev_i) % z1 * s...]
    all_to_all x1, starting transfers between devices: 3.5 us -> 16.1 us  [local(): lax.all_to_all(split_qr, 'land', split_axis=1, concat_axis=3, tiled=True)]
    broadcast_in_dim x0 -> x1, local copies, waits for them, and re-layouts: none -> 6.65 us  [_touch_slices(): jnp.zeros((*tile_in.shape[:1], z1 * side_arr, *tile_in.shape[2:]), tile_i...]
    ppermute x0 -> x3, starting transfers between devices: none -> 5.04 us  [the longest x2 3.02 us: _touch_slices(): after = ppermute(after, 'land', all_rows)]
    unnamed x17 -> x19, local copies, waits for them, and re-layouts: 8.18 us -> 6.34 us
  transfers between devices with their start and end apart: 4 -> 6, of which waited for: 2 -> 2; matrix products, arithmetic and copies ran while one was open for 24% -> 27% of each run, Pallas kernels for 0% -> 0%
where the time goes in v1:
time: 337 us; the launch traced here: 336 us
  waiting for transfers between devices  138 us (41%)
  blocking collectives  103 us (31%)
  local copies, waits for them, and re-layouts  46.5 us (14%)
  starting transfers between devices  27.7 us (8%)
  matrix products  18.9 us (6%)
    ppermute x2, waiting for transfers between devices, _touch_slices(): after = ppermute(after, 'land', all_rows)  88.7 us
    unnamed x3, blocking collectives  65.9 us
    all_to_all x1, waiting for transfers between devices, local(): lax.all_to_all(split_ex, 'land', split_axis=1, concat_axis=3, tiled=True)  49 us
    all_gather x1, blocking collectives, local(): all_queries = lax.all_gather(query_white, 'layer', axis=0, tiled=True)  26 us
    dot_general x3, matrix products, contract_rows(): lax.dot_general(rows, piece, (((1,), (1,)), ((), ())), preferred_element_...  18.7 us
    all_to_all x1, starting transfers between devices, local(): lax.all_to_all(split_qr, 'land', split_axis=1, concat_axis=3, tiled=True)  16.1 us
    reshape x2, local copies, waits for them, and re-layouts, local(): split_ex = gradients.reshape(n_layer, n_land, rows_each, width)  11.3 us
    dynamic_update_slice x2, local copies, waits for them, and re-layouts, _touch_slices(): lax.dynamic_update_slice_in_dim(part_now, after, (outer - dev_i) % z1 * s...  9.39 us
  transfers between devices with their start and end apart: 6, of which 2 were waited for; matrix products, arithmetic and copies ran while one was open for 27% of the time, Pallas kernels for 0%

profile of v1, /device:TPU:0, one launch (start us, length us, event | category | flops | bytes accessed | tf_op | source)
XLA Modules:
  0.0 336.2 jit_solution(8066812109803627216)
XLA Ops:
  0.5 2.0 collective-permute-start.1
  2.6 88.7 %collective-permute-done = bf16[1024,2048]{1,0:T(8,128)(2,1)} collective-permute-done((bf16[1024,2048]{1,0:T(8,128)(2,1)}, bf16[1024,2048]{1,0:T(8,128)(2,1)}, u32[]{:S(2)}, u32[]{:S(2)}) %collective-permute-start) | collective-permute-done | bytes 4194336 | tf_op jit(solution)/shard_map/ppermute | solution.py:45
  91.3 2.5 collective-permute-start.2
  93.8 5.0 %reshape.19 = bf16[8,4,30,2048]{3,2,1,0:T(8,128)(2,1)} reshape(bf16[960,2048]{1,0:T(8,128)(2,1)} %param.4) | data formatting | bytes 7864320 | tf_op jit(solution)/shard_map/reshape | solution.py:26
  98.8 6.2 %copy.9 = bf16[8,4,30,2048]{3,0,2,1:T(8,128)(2,1)} copy(bf16[8,4,30,2048]{3,2,1,0:T(8,128)(2,1)} %reshape.19) | data formatting | bytes 7864320 | tf_op jit(solution)/shard_map/reshape | solution.py:26
  105.0 4.8 %all-to-all-start.1 = ((bf16[8,4,30,2048]{3,0,2,1:T(8,128)(2,1)}), bf16[8,4,30,2048]{3,0,2,1:T(8,128)(2,1)}, u32[]{:S(2)}, u32[]{:S(2)}) async-start(bf16[8,4,30,2048]{3,0,2,1:T(8,128)(2,1)} %copy.9), calls=%async_computation.1 | async-start | bytes 7864320 | tf_op jit(solution)/shard_map/all_to_all | solution.py:29
  113.2 6.6 %broadcast_in_dim.3 = bf16[1024,8192]{1,0:T(8,128)(2,1)} broadcast(bf16[]{:T(256)} %constant.30.clone.1), dimensions={} | broadcast | bytes 16777218 | tf_op jit(solution)/shard_map/broadcast_in_dim | solution.py:40
  119.9 2.2 constant_dynamic-update-slice_fusion.3
  122.1 49.0 %all-to-all-done.1 = bf16[8,4,30,2048]{3,0,2,1:T(8,128)(2,1)} async-done(((bf16[8,4,30,2048]{3,0,2,1:T(8,128)(2,1)}), bf16[8,4,30,2048]{3,0,2,1:T(8,128)(2,1)}, u32[]{:S(2)}, u32[]{:S(2)}) %all-to-all-start.1) | async-done | bytes 3932192 | tf_op jit(solution)/shard_map/all_to_all | solution.py:29
  171.1 16.1 %all-to-all-start = ((bf16[8,4,1,2048]{3,0,2,1:T(8,128)(2,1)}), bf16[8,4,1,2048]{3,0,2,1:T(8,128)(2,1)S(1)}, u32[]{:S(2)}, u32[]{:S(2)}) async-start(bf16[8,4,1,2048]{3,0,2,1:T(8,128)(2,1)} %copy.8), calls=%async_computation | async-start | bytes 262144 | tf_op jit(solution)/shard_map/all_to_all | solution.py:30
  187.2 5.1 %copy.10 = bf16[8,1,30,4,2048]{4,3,2,0,1:T(4,128)(2,1)S(1)} copy(bf16[8,1,30,4,2048]{4,0,2,3,1:T(8,128)(2,1)} %bitcast.5) | data formatting | bytes 7864320 | tf_op jit(solution)/shard_map/all_to_all | solution.py:29
  192.4 4.1 %copy.12 = bf16[30,8,4,2048]{3,1,2,0:T(8,128)(2,1)S(1)} copy(bf16[30,8,4,2048]{3,2,1,0:T(4,128)(2,1)S(1)} %bitcast.33) | data formatting | bytes 7864320
  196.5 4.7 %constant_dynamic-update-slice_fusion.2 = bf16[1024,8192]{1,0:T(8,128)(2,1)} fusion(bf16[1024,8192]{1,0:T(8,128)(2,1)} %constant_dynamic-update-slice_fusion.3, bf16[1024,2048]{1,0:T(8,128)(2,1)} %collective-permute-done, s32[]{:T(128)S(6)} %select_n.29), kind=kLoop, calls=%fused_computation.17 | loop fusion | bytes 8388612 | tf_op jit(solution)/shard_map/dynamic_update_slice | solution.py:46
  201.2 4.7 %constant_dynamic-update-slice_fusion.1 = bf16[1024,8192]{1,0:T(8,128)(2,1)} fusion(bf16[1024,8192]{1,0:T(8,128)(2,1)} %constant_dynamic-update-slice_fusion.2, bf16[1024,2048]{1,0:T(8,128)(2,1)} %collective-permute-done.1, s32[]{:T(128)S(6)} %select_n.31), kind=kLoop, calls=%fused_computation.16 | loop fusion | bytes 8388612 | tf_op jit(solution)/shard_map/dynamic_update_slice | solution.py:51
  205.9 4.7 %constant_dynamic-update-slice_fusion = bf16[1024,8192]{1,0:T(8,128)(2,1)} fusion(bf16[1024,8192]{1,0:T(8,128)(2,1)} %constant_dynamic-update-slice_fusion.1, bf16[1024,2048]{1,0:T(8,128)(2,1)} %collective-permute-done.2, s32[]{:T(128)S(6)} %select_n.33), kind=kLoop, calls=%fused_computation.15 | loop fusion | bytes 8388612 | tf_op jit(solution)/shard_map/dynamic_update_slice | solution.py:46
  210.6 8.2 %fusion.1 = bf16[240,1024]{1,0:T(8,128)(2,1)S(1)} fusion(bf16[1024,8192]{1,0:T(8,128)(2,1)} %constant_dynamic-update-slice_fusion, bf16[240,8192]{1,0:T(8,128)(2,1)S(1)} %bitcast.34), kind=kOutput, calls=%fused_computation.1 | convolution fusion | flops 4026777600 | bytes 21200896 | tf_op jit(solution)/shard_map/dot_general | solution.py:11
  218.8 25.1 %fusion = bf16[32,1024]{1,0:T(8,128)(2,1)S(1)} fusion(bf16[240,1024]{1,0:T(8,128)(2,1)S(1)} %fusion.1), kind=kCustom, calls=%all-reduce-scatter | all-reduce-scatter fusion | flops 262145 | bytes 557568
  243.9 1.8 collective-permute-start.3
  245.7 10.2 %fusion.3 = bf16[8,1024]{1,0:T(8,128)(2,1)S(1)} fusion(bf16[1024,8192]{1,0:T(8,128)(2,1)} %constant_dynamic-update-slice_fusion, bf16[8,8192]{1,0:T(8,128)(2,1)S(1)} %bitcast.35), kind=kOutput, calls=%fused_computation.5 | convolution fusion | flops 134225920 | bytes 16924672 | tf_op jit(solution)/shard_map/dot_general | solution.py:11
  255.8 33.7 %all-reduce = bf16[8,1024]{1,0:T(8,128)(2,1)S(1)} all-reduce(bf16[8,1024]{1,0:T(8,128)(2,1)S(1)} %fusion.3), channel_id=2, replica_groups=mesh['layer'=8,'land'=4] {'layer'}, use_global_device_ids=true, to_apply=%region_0.1.clone | all-reduce | flops 8192 | bytes 32768
  290.1 5.2 %all-gather = bf16[4,1,1024]{2,1,0:T(2,128)(2,1)S(1)} all-gather(bf16[1,1,1024]{2,1,0:T(2,128)(2,1)S(1)} %dynamic-slice_bitcast_fusion.1), channel_id=1, replica_groups=mesh['layer'=8,'land'=4] {'land'}, dimensions={0}, use_global_device_ids=true | all-gather | bytes 10240 | tf_op jit(solution)/shard_map/all_gather | solution.py:67
  295.5 26.0 %all-gather.1 = bf16[8,4,256]{2,1,0:T(4,128)(2,1)S(1)} all-gather(bf16[1,4,256]{2,1,0:T(4,128)(2,1)S(1)} %fusion.6), channel_id=1, replica_groups=mesh['layer'=8,'land'=4] {'layer'}, dimensions={0}, use_global_device_ids=true | all-gather | bytes 18432 | tf_op jit(solution)/shard_map/all_gather | solution.py:75
  321.8 6.2 %all-gather.2 = bf16[4,30,1024]{2,1,0:T(8,128)(2,1)S(1)} all-gather(bf16[1,30,1024]{2,1,0:T(8,128)(2,1)S(1)} %dynamic-slice_bitcast_fusion), channel_id=1, replica_groups=mesh['layer'=8,'land'=4] {'land'}, dimensions={0}, use_global_device_ids=true | all-gather | bytes 307200 | tf_op jit(solution)/shard_map/all_gather | solution.py:66
  328.4 7.2 %all-reduce.2 = bf16[32,120]{1,0:T(8,128)(2,1)S(1)} all-reduce(bf16[32,120]{1,0:T(8,128)(2,1)S(1)} %fusion.5), channel_id=4, replica_groups=mesh['layer'=8,'land'=4] {'land'}, use_global_device_ids=true, to_apply=%region_2.3.clone | all-reduce | flops 3840 | bytes 15360
  (28 shorter events, 4.7 us)
Async XLA Ops:
  0.0 295.3 %copy-start = (bf16[1024,256]{1,0:T(8,128)(2,1)S(1)}, bf16[1024,256]{1,0:T(8,128)(2,1)}, u32[]{:S(2)}) copy-start(bf16[1024,256]{1,0:T(8,128)(2,1)} %param.7) | copy-start | bytes 1572868
  0.0 110.8 %copy-start.4 = (u32[32]{0:T(128)S(1)}, u32[32]{0:T(128)}, u32[]{:S(2)}) copy-start(u32[32]{0:T(128)} %constant.51) | copy-start | bytes 388
  0.0 111.3 %copy-start.3 = (u32[32]{0:T(128)S(1)}, u32[32]{0:T(128)}, u32[]{:S(2)}) copy-start(u32[32]{0:T(128)} %constant.43) | copy-start | bytes 388
  0.0 109.9 %copy-start.2 = (bf16[32,2048]{1,0:T(8,128)(2,1)S(1)}, bf16[32,2048]{1,0:T(8,128)(2,1)}, u32[]{:S(2)}) copy-start(bf16[32,2048]{1,0:T(8,128)(2,1)} %param.5) | copy-start | bytes 393220
  0.0 91.3 %collective-permute-start = (bf16[1024,2048]{1,0:T(8,128)(2,1)}, bf16[1024,2048]{1,0:T(8,128)(2,1)}, u32[]{:S(2)}, u32[]{:S(2)}) collective-permute-start(bf16[1024,2048]{1,0:T(8,128)(2,1)} %param.6), channel_id=1, source_target_pairs={{0,1},{1,2},{2,3},{3,0},{4,5},{5,6},{6,7},{7,4},{8,9},{9,10},{10,1... | collective-permute-start | bytes 12582920 | tf_op jit(solution)/shard_map/ppermute | solution.py:45
  0.5 200.7 %collective-permute-start.1 = (bf16[1024,2048]{1,0:T(8,128)(2,1)}, bf16[1024,2048]{1,0:T(8,128)(2,1)}, u32[]{:S(2)}, u32[]{:S(2)}) collective-permute-start(bf16[1024,2048]{1,0:T(8,128)(2,1)} %param.6), channel_id=1, source_target_pairs={{0,3},{1,0},{2,1},{3,2},{4,7},{5,4},{6,5},{7,6},{8,11},{9,8},{10,9... | collective-permute-start | bytes 12582920 | tf_op jit(solution)/shard_map/ppermute | solution.py:50
  91.3 114.6 %collective-permute-start.2 = (bf16[1024,2048]{1,0:T(8,128)(2,1)}, bf16[1024,2048]{1,0:T(8,128)(2,1)}, u32[]{:S(2)}, u32[]{:S(2)}) collective-permute-start(bf16[1024,2048]{1,0:T(8,128)(2,1)} %collective-permute-done), channel_id=1, source_target_pairs={{0,1},{1,2},{2,3},{3,0},{4,5},{5,6},{6,7},{7,4},{8,9},{9,10},{10,1... | collective-permute-start | bytes 12582920 | tf_op jit(solution)/shard_map/ppermute | solution.py:45
  105.0 66.1 %all-to-all-start.1 = ((bf16[8,4,30,2048]{3,0,2,1:T(8,128)(2,1)}), bf16[8,4,30,2048]{3,0,2,1:T(8,128)(2,1)}, u32[]{:S(2)}, u32[]{:S(2)}) async-start(bf16[8,4,30,2048]{3,0,2,1:T(8,128)(2,1)} %copy.9), calls=%async_computation.1 | async-start | bytes 7864320 | tf_op jit(solution)/shard_map/all_to_all | solution.py:29
  113.2 6.7 %copy-start.1 = (bf16[1024,2048]{1,0:T(8,128)(2,1)S(1)}, bf16[1024,2048]{1,0:T(8,128)(2,1)}, u32[]{:S(2)}) copy-start(bf16[1024,2048]{1,0:T(8,128)(2,1)} %param.6) | copy-start | bytes 12582916
  171.1 74.5 %all-to-all-start = ((bf16[8,4,1,2048]{3,0,2,1:T(8,128)(2,1)}), bf16[8,4,1,2048]{3,0,2,1:T(8,128)(2,1)S(1)}, u32[]{:S(2)}, u32[]{:S(2)}) async-start(bf16[8,4,1,2048]{3,0,2,1:T(8,128)(2,1)} %copy.8), calls=%async_computation | async-start | bytes 262144 | tf_op jit(solution)/shard_map/all_to_all | solution.py:30
  243.9 77.7 %collective-permute-start.3 = (bf16[14,1024]{1,0:T(8,128)(2,1)S(1)}, bf16[14,1024]{1,0:T(8,128)(2,1)S(1)}, u32[]{:S(2)}, u32[]{:S(2)}) collective-permute-start(bf16[14,1024]{1,0:T(8,128)(2,1)S(1)} %slice), channel_id=1, source_target_pairs={{0,4},{4,8},{8,12},{12,16},{16,20},{20,24},{24,28},{1,5},{5,9},{9,... | collective-permute-start | bytes 86024
